TPU v7x, 256 devices: a whole 4x4x8 slice. The times are simulated.
256 devices in a mesh: ctx: 32 (over z_lo, x, core), wt: 8 (over y, z_hi).
Axes of the slice: x: 4, y: 4, z: 8 (z_hi: 2, z_lo: 4; z = z_hi * 4 + z_lo), core: 2. Of those that a mesh axis runs over, the one named last changes fastest.
Arguments:
- patches: bfloat16 [16384, 1280], P('ctx'), may hold values from -6 to 6
- vit_gain: float32 [1280], replicated, may hold values from 0.5 to 1.5
- vit_codes: bfloat16 [1280, 3, 1280], P(None, None, 'wt'), may hold values from -1 to 1
- vit_scales: bfloat16 [8], P('wt'), may hold values from 0.5 to 2
- vit_bias: float32 [3, 1280], P(None, 'wt'), may hold values from -3 to 3
- window_ids: int32 [16384], P('ctx'), may hold values from 63 to 16383, as said below
- merger_codes: bfloat16 [4, 1280, 8192], P(None, 'wt', 'ctx'), may hold values from -0.078125 to 0.078125
- merger_scales: bfloat16 [1, 8, 8192], P(None, 'wt', 'ctx'), may hold values from 0.5 to 2
- merger_bias: float32 [8192], P('wt'), may hold values from -3 to 3
- positions: int32 [4096], P('ctx'), may hold values from 0 to 16383, as said below
- text_embed: bfloat16 [16384, 8192], P('ctx', 'wt'), may hold values from -6 to 6
- norm_gain: float32 [8192], P('wt'), may hold values from 0.5 to 1.5
- llm_codes: bfloat16 [8192, 8, 768], P('wt', None, 'ctx'), may hold values from -1 to 1
- llm_scales: bfloat16 [8, 8, 768], P('wt', None, 'ctx'), may hold values from 0.5 to 2
- llm_bias: float32 [8, 768], P('wt'), may hold values from -3 to 3
- segments: int32 [16384], P('ctx'), may hold values from 0 to 15, never falling along the last dimension, each value on 1 to 2048 neighbouring positions
Outputs:
- attention_out: bfloat16 [16384, 4096], P('ctx', 'wt')
Inputs may be any that keep to these rules, and one draw needn't show every extreme that they name: `window_ids`: windows are runs of consecutive patches of at most 64, never crossing a block of 512 patches; patches of one window share the id, different windows have different ids. `positions`: distinct. The 128 entries of one aligned block (one device's merged tokens) put at most 8 into any one block of 512 positions, and exactly 8 into some block. `segments`: never falling; each run of equal ids is at most 2048 positions long.
All inputs are finite; a program needn't handle non-finite values.
Results may differ from a plain program's by a relative error of at most 0.025.
Values may be sent and summed in bfloat16 or wider, within the bound.
A program may use at most 128 MiB of HBM per device.

v0:
```python
import jax
import jax.numpy as jnp
from jax import lax
from jax.sharding import PartitionSpec as P

VHD = 80
D = 8192
KVH = 8
HD = 128
GROUP = 4
MERGE = 4
REACH = 4


VIT_EPS = 1e-06
RMS_EPS = 1e-06
ROPE_BASE = 1000000.0
FILL_LOW = -1e30


def in_blocks(x, dim, peers):
    before, after = (x.shape[:dim], x.shape[dim + 1 :])
    return jnp.moveaxis(x.reshape(*before, peers, -1, *after), dim, 0)


def summed_on_arrival(x, axis, dim):
    parts = in_blocks(x, dim, lax.axis_size(axis))
    arrived = lax.all_to_all(parts, axis, split_axis=0, concat_axis=0, tiled=True)
    return arrived.astype(jnp.float32).sum(axis=0)


def passed_along(value, axis, steps):
    count = lax.axis_size(axis)
    leading, last = (max(0, -steps), min(count, count - steps))
    return lax.ppermute(value, axis, [(source, source + steps) for source in range(leading, last)])


def softmax_rows(scores, allowed):
    masked = jnp.where(allowed, scores, FILL_LOW)
    highest = jnp.max(masked, axis=-1, keepdims=True)
    raised = jnp.exp(masked - highest)
    return raised / jnp.sum(raised, axis=-1, keepdims=True)


def vision_norm_rows(patches, vit_gain):
    values = patches.astype(jnp.float32)
    mean_square = jnp.mean(values * values, axis=1, keepdims=True)
    return (values * lax.rsqrt(mean_square + VIT_EPS) * vit_gain).astype(jnp.bfloat16)


def window_attention(normed, weight_block, bias_block, window_ids):
    row_count = normed.shape[0]
    packed = jnp.dot(
        normed, weight_block.reshape(normed.shape[1], -1), preferred_element_type=jnp.float32
    )
    triple = (packed.reshape(row_count, 3, -1) + bias_block).astype(jnp.bfloat16)
    heads_here = triple.shape[2] // VHD
    queries = triple[:, 0].reshape(row_count, heads_here, VHD)
    keys_here = triple[:, 1].reshape(row_count, heads_here, VHD)
    values_here = triple[:, 2].reshape(row_count, heads_here, VHD)
    scores = jnp.einsum(
        "qhd,khd->hqk", queries, keys_here, preferred_element_type=jnp.float32
    ) * VHD ** (-0.5)
    allowed = window_ids[:, None] == window_ids[None, :]
    softmaxed = softmax_rows(scores, allowed[None]).astype(jnp.bfloat16)
    blended = jnp.einsum("hqk,khd->qhd", softmaxed, values_here, preferred_element_type=jnp.float32)
    return blended.astype(jnp.bfloat16).reshape(row_count, -1)


def rope_tables(first, length):
    places = (first + jnp.arange(length, dtype=jnp.int32)).astype(jnp.float32)
    frequency = ROPE_BASE ** (-jnp.arange(0, HD, 2).astype(jnp.float32) / HD)
    angles = places[:, None] * frequency[None, :]
    angles = jnp.concatenate([angles, angles], axis=1)
    return (jnp.cos(angles), jnp.sin(angles))


def rotary(inputs, cosine, sine):
    halfway = inputs.shape[-1] // 2
    turned = jnp.concatenate([-inputs[..., halfway:], inputs[..., :halfway]], axis=-1)
    return inputs * cosine + turned * sine


def split_heads(triple, cosine, sine):
    row_count, group_count = (triple.shape[0], triple.shape[1])
    queries = triple[:, :, : GROUP * HD].reshape(row_count, group_count, GROUP, HD)
    queries = rotary(queries, cosine[:, None, None, :], sine[:, None, None, :]).astype(jnp.bfloat16)
    keys_rot = rotary(
        triple[:, :, GROUP * HD : (GROUP + 1) * HD], cosine[:, None, :], sine[:, None, :]
    ).astype(jnp.bfloat16)
    values_cut = triple[:, :, (GROUP + 1) * HD :].astype(jnp.bfloat16)
    return (queries, keys_rot, values_cut)


def merge_project(features, merger_codes, merger_scales, merger_bias):
    row_count = features.shape[0]
    flat = features.reshape(row_count, -1)
    codes_piece = lax.all_gather(merger_codes, "ctx", axis=2, tiled=True)
    scale_piece = lax.all_gather(merger_scales, "ctx", axis=2, tiled=True)
    width = codes_piece.shape[2]
    dequant = (codes_piece.astype(jnp.float32) * scale_piece.astype(jnp.float32)).astype(
        jnp.bfloat16
    )
    product = jnp.dot(flat, dequant.reshape(-1, width), preferred_element_type=jnp.float32)
    mine = summed_on_arrival(product.astype(jnp.bfloat16), "wt", 1)
    return (mine + merger_bias).astype(jnp.bfloat16)


def route_tokens(values, positions, span):
    owners = lax.axis_size("ctx")
    items = values.shape[0]
    capacity = 2 * positions.shape[0] // owners
    target = positions // span
    item_order = jnp.arange(items, dtype=jnp.int32)
    before = (target[None, :] == target[:, None]) & (item_order[None, :] < item_order[:, None])
    ranks = jnp.sum(before.astype(jnp.int32), axis=1)
    slots = target * capacity + ranks
    table = slots[None, :] == jnp.arange(owners * capacity, dtype=jnp.int32)[:, None]
    packed = jnp.dot(table.astype(jnp.bfloat16), values, preferred_element_type=jnp.float32).astype(
        jnp.bfloat16
    )
    labels = jnp.sum(jnp.where(table, positions[None, :] + 1, 0), axis=1) - 1
    return (
        lax.all_to_all(packed, "ctx", split_axis=0, concat_axis=0, tiled=True),
        lax.all_to_all(labels, "ctx", split_axis=0, concat_axis=0, tiled=True),
    )


def place_tokens(text_embed, arrived, labels, first):
    local = labels - first
    table = local[None, :] == jnp.arange(text_embed.shape[0], dtype=jnp.int32)[:, None]
    filled = jnp.dot(
        table.astype(jnp.bfloat16), arrived, preferred_element_type=jnp.float32
    ).astype(jnp.bfloat16)
    covered = jnp.any(table, axis=1)
    return jnp.where(covered[:, None], filled, text_embed)


def on_device(
    patches,
    vit_gain,
    vit_codes,
    vit_scales,
    vit_bias,
    window_ids,
    merger_codes,
    merger_scales,
    merger_bias,
    positions,
    text_embed,
    norm_gain,
    llm_codes,
    llm_scales,
    llm_bias,
    segments,
):
    early_codes, early_scales = (
        lax.all_gather(llm_codes, "ctx", axis=2, tiled=True),
        lax.all_gather(llm_scales, "ctx", axis=2, tiled=True),
    )
    row_count = text_embed.shape[0]
    first = lax.axis_index("ctx") * row_count
    normed_patches = vision_norm_rows(patches, vit_gain)
    vit_weight = (vit_codes.astype(jnp.float32) * vit_scales.astype(jnp.float32)[0]).astype(
        jnp.bfloat16
    )
    attended = window_attention(normed_patches, vit_weight, vit_bias, window_ids)
    token_count = positions.shape[0]
    features = attended.reshape(token_count, MERGE, -1)
    projected = merge_project(features, merger_codes, merger_scales, merger_bias)
    embedded, labels = route_tokens(projected, positions, row_count)
    hidden = place_tokens(text_embed, embedded, labels, first)
    values = hidden.astype(jnp.float32)
    squares = lax.psum(jnp.sum(values * values, axis=1), "wt")
    normed = (values * lax.rsqrt(squares[:, None] / D + RMS_EPS) * norm_gain).astype(jnp.bfloat16)
    local_rows = normed.shape[1]
    dequant = (early_codes.astype(jnp.float32) * early_scales.astype(jnp.float32)).astype(
        jnp.bfloat16
    )
    partial_value = jnp.dot(
        normed, dequant.reshape(local_rows, -1), preferred_element_type=jnp.float32
    ).reshape(row_count, KVH, -1)
    triple = (
        lax.psum_scatter(
            partial_value.astype(jnp.bfloat16), "wt", scatter_dimension=1, tiled=True
        ).astype(jnp.float32)
        + llm_bias
    )
    cosine, sine = rope_tables(first, row_count)
    queries, keys_rot, values_cut = split_heads(triple, cosine, sine)
    own = (keys_rot, values_cut, segments)
    arrivals = [own]
    for distance in range(1, REACH + 1):
        arrivals.append(passed_along((own[0], own[1], own[2]), "ctx", distance))
    keys_all = jnp.concatenate([arrival[0] for arrival in arrivals], axis=0)
    values_all = jnp.concatenate([arrival[1] for arrival in arrivals], axis=0)
    key_segments = jnp.concatenate([arrival[2] for arrival in arrivals], axis=0)
    key_places = jnp.concatenate(
        [
            first - distance * row_count + jnp.arange(row_count, dtype=jnp.int32)
            for distance in range(REACH + 1)
        ],
        axis=0,
    )
    query_places = first + jnp.arange(row_count, dtype=jnp.int32)
    allowed = (
        (segments[:, None] == key_segments[None, :])
        & (key_places[None, :] <= query_places[:, None])
        & (key_places[None, :] >= 0)
    )
    scores = jnp.einsum(
        "qjd,kd->jqk", queries[:, 0], keys_all[:, 0], preferred_element_type=jnp.float32
    ) * HD ** (-0.5)
    softmaxed = softmax_rows(scores, allowed[None]).astype(jnp.bfloat16)
    blended = jnp.einsum(
        "jqk,kd->qjd", softmaxed, values_all[:, 0], preferred_element_type=jnp.float32
    )
    outputs = blended.astype(jnp.bfloat16).reshape(row_count, -1)
    return outputs


def solution(mesh):
    in_specs = (
        P("ctx", None),
        P(),
        P(None, None, "wt"),
        P("wt"),
        P(None, "wt"),
        P("ctx"),
        P(None, "wt", "ctx"),
        P(None, "wt", "ctx"),
        P("wt"),
        P("ctx"),
        P("ctx", "wt"),
        P("wt"),
        P("wt", None, "ctx"),
        P("wt", None, "ctx"),
        P("wt", None),
        P("ctx"),
    )
    out_specs = P("ctx", "wt")
    return jax.shard_map(
        on_device, mesh=mesh, in_specs=in_specs, out_specs=out_specs, check_vma=False
    )
```

profile of v0, /device:TPU:3, one launch (start us, length us, event | category | flops | bytes accessed | tf_op | source)
XLA Modules:
  0.0 531.8 jit_solution(2838187777075380373)
XLA Ops:
  6.5 0.7 all-gather.3.cloned.1.call-update
  8.7 1.6 fusion.14
  10.3 1.0 broadcast_compare_fusion
  11.3 2.2 fusion.29
  13.6 1.0 fusion.82
  14.6 1.2 fusion.36
  16.2 40.4 %all_gather.13 = bf16[1,1,8192]{2,1,0:T(2,128)(2,1)S(1)} all-gather(bf16[1,1,256]{2,1,0:T(2,128)(2,1)S(1)} %copy-done.8), channel_id=1, replica_groups=mesh['ctx'=32,'wt'=8] {'ctx'}, dimensions={2}, use_global_device_ids=true | all-gather | bytes 16896 | tf_op jit(solution)/shard_map/all_gather | solution.py:99
  56.7 51.3 %all-gather.3.cloned.1.call-done = bf16[4,160,8192]{2,1,0:T(8,128)(2,1)} async-done(((bf16[4,160,256]{2,1,0:T(8,128)(2,1)}), bf16[4,160,8192]{2,1,0:T(8,128)(2,1)}) %all-gather.3.cloned.1.call-update) | async-done | bytes 10485776 | tf_op jit(solution)/shard_map/all_gather | solution.py:98
  108.0 6.2 %multiply_convert_fusion.1 = bf16[4,160,8192]{2,1,0:T(8,128)(2,1)S(1)} fusion(bf16[4,160,8192]{2,1,0:T(8,128)(2,1)} %all-gather.3.cloned.1.call-done, f32[8192]{0:T(1024)S(1)} %bitcast.110), kind=kLoop, calls=%fused_computation.6 | loop fusion | flops 15728640 | bytes 21004288 | tf_op jit(solution)/shard_map/convert_element_type | solution.py:101
  114.1 2.0 convolution_convert_fusion
  116.1 1.5 copy.64
  117.6 7.9 %all-to-all-start.1 = ((bf16[8,128,1024]{2,1,0:T(8,128)(2,1)}), bf16[8,128,1024]{2,1,0:T(8,128)(2,1)S(1)}, u32[]{:S(2)}, u32[]{:S(2)}) async-start(bf16[8,128,1024]{2,1,0:T(8,128)(2,1)} %bitcast.102), calls=%async_computation.1 | async-start | bytes 4194304 | tf_op jit(solution)/shard_map/all_to_all | solution.py:28
  126.6 36.0 %all-to-all-done.1 = bf16[8,128,1024]{2,1,0:T(8,128)(2,1)S(1)} async-done(((bf16[8,128,1024]{2,1,0:T(8,128)(2,1)}), bf16[8,128,1024]{2,1,0:T(8,128)(2,1)S(1)}, u32[]{:S(2)}, u32[]{:S(2)}) %all-to-all-start.1) | async-done | bytes 2097184 | tf_op jit(solution)/shard_map/all_to_all | solution.py:28
  162.6 43.8 %all-to-all-start = ((s32[32,8,1]{1,2,0:T(1,128)}), s32[32,8,1]{1,2,0:T(1,128)S(1)}, u32[]{:S(2)}, u32[]{:S(2)}) async-start(s32[32,8,1]{1,2,0:T(1,128)} %bitcast), calls=%async_computation | async-start | bytes 32768 | tf_op jit(solution)/shard_map/all_to_all | solution.py:125
  206.8 1.1 fusion.32
  207.9 5.2 all-to-all-done
  213.1 4.9 all-to-all-start.2
  218.2 54.7 %all_gather.15 = bf16[1,8,768]{1,0,2:T(2,128)(2,1)S(1)} all-gather(bf16[1,8,24]{1,0,2:T(2,128)(2,1)S(1)} %copy.42), channel_id=1, replica_groups=mesh['ctx'=32,'wt'=8] {'ctx'}, dimensions={2}, use_global_device_ids=true | all-gather | bytes 12672 | tf_op jit(solution)/shard_map/all_gather | solution.py:159
  274.4 20.6 %psum.7 = f32[512]{0:T(512)S(1)} all-reduce(f32[512]{0:T(512)S(1)} %get-tuple-element.24), channel_id=1, replica_groups=mesh['ctx'=32,'wt'=8] {'wt'}, use_global_device_ids=true, to_apply=%region_8.9 | all-reduce | flops 512 | bytes 4096 | tf_op jit(solution)/shard_map/psum | solution.py:174
  294.9 11.6 %fusion.11 = bf16[512,8,768]{2,0,1:T(8,128)(2,1)} fusion(bf16[1024,8,768]{0,2,1:T(8,128)(2,1)} %all-gather.5.cloned.1.call-done, f32[8,768]{1,0:T(8,128)S(1)} %copy.43, bf16[512,1024]{1,0:T(8,128)(2,1)S(1)} %get-tuple-element.25, f32[1024]{0:T(1024)S(1)} %copy-done.12, f32[512]{0:T(512)S(1)} %add_rsqrt_fusion), kind=kOutput, calls=%fused_computation.18 | convolution fusion | flops 6466568192 | bytes 19953664 | tf_op jit(solution)/shard_map/dot_general | solution.py:180
  307.2 4.1 collective-permute-start.4
  311.3 1.9 collective-permute-start.5
  313.3 1.9 collective-permute-start.6
  315.2 1.4 collective-permute-start.7
  316.8 1.1 fusion.66
  318.2 1.4 mul.219
  319.7 3.5 and_and_fusion
  323.2 130.1 %reduce-scatter.2.cloned.1.call-done = bf16[512,1,768]{2,0,1:T(8,128)(2,1)} async-done(((bf16[512,8,768]{2,0,1:T(8,128)(2,1)}), bf16[512,1,768]{2,0,1:T(8,128)(2,1)}) %reduce-scatter.2.cloned.1.call-update) | async-done | bytes 786448 | tf_op jit(solution)/shard_map/reduce_scatter | solution.py:184
  453.3 1.2 convert_add_fusion
  454.7 1.9 constant_dynamic-update-slice_fusion.4
  456.6 9.9 %collective-permute-start = (bf16[512,1,128]{2,0,1:T(8,128)(2,1)}, bf16[512,1,128]{2,0,1:T(8,128)(2,1)S(1)}, u32[]{:S(2)}, u32[]{:S(2)}) collective-permute-start(bf16[512,1,128]{2,0,1:T(8,128)(2,1)} %get-tuple-element.6), channel_id=1, source_target_pairs={{0,8},{8,16},{16,24},{24,32},{32,40},{40,48},{48,56},{56,64},{64,7... | collective-permute-start | bytes 393224 | tf_op jit(solution)/shard_map/ppermute | solution.py:35
  466.5 2.8 collective-permute-start.1
  469.3 2.9 collective-permute-start.2
  472.2 1.1 slice.50
  473.3 3.4 collective-permute-start.8
  476.7 3.1 collective-permute-start.9
  479.8 1.6 reshape.464
  482.0 1.6 maximum_multiply_fusion
  483.7 2.6 mul.223
  486.3 1.5 add_convert_fusion
  487.9 3.6 collective-permute-start.10
  491.5 1.6 constant_dynamic-update-slice_fusion.10
  493.1 2.3 collective-permute-start.11
  495.4 1.6 constant_dynamic-update-slice_fusion.9
  497.0 4.7 collective-permute-start.3
  503.0 12.6 %fusion.83 = (f32[4,512]{1,0:T(4,128)S(1)}, f32[4,512,2560]{1,2,0:T(8,128)}) fusion(pred[512,2560]{0,1:T(8,128)(4,1)S(1)} %copy-done.2, bf16[2560,1,128]{2,0,1:T(8,128)(2,1)} %constant_dynamic-update-slice_fusion.7, bf16[512,4,128]{2,1,0:T(4,128)(2,1)S(1)} %convert_element_type.133), kind=kOutput, calls=%fused_computation.137 | convolution fusion | flops 1363151360 | bytes 23470080 | tf_op jit(solution)/shard_map/sub | solution.py:41
  515.7 8.5 %fusion.28 = bf16[128,4,512]{2,0,1:T(8,128)(2,1)S(1)} fusion(f32[4,512,2560]{1,2,0:T(8,128)} %get-tuple-element.27, f32[4,512]{1,0:T(4,128)S(1)} %get-tuple-element.26, bf16[2560,1,128]{2,0,1:T(8,128)(2,1)S(1)} %constant_dynamic-update-slice_fusion), kind=kOutput, calls=%fused_computation.44 | convolution fusion | flops 1352925184 | bytes 22159360 | tf_op jit(solution)/shard_map/jqk,kd->qjd/dot_general | solution.py:215
  524.3 1.0 copy.47
  (94 shorter events, 7.6 us)
Async XLA Ops:
  6.5 4.8 copy-start.1
  6.5 4.8 copy-start.10
  6.5 4.8 copy-start.11
  6.5 101.4 %all-gather.3.cloned.1.call-start = ((), (), s32[]{:S(2)}) async-start(), calls=%async_computation.4 | async-start | bytes 10813440 | tf_op jit(solution)/shard_map/all_gather | solution.py:98
  7.3 287.7 %all-gather.5.cloned.1.call-start = ((), (), s32[]{:S(2)}) async-start(), calls=%async_computation.5 | async-start | bytes 12976128 | tf_op jit(solution)/shard_map/all_gather | solution.py:158
  14.6 1.6 copy-start.8
  117.6 7.9 %copy-start.13 = (s32[128]{0:T(128)S(1)}, s32[128]{0:T(128)}, u32[]{:S(2)}) copy-start(s32[128]{0:T(128)} %param.25) | copy-start | bytes 1540
  117.6 45.0 %all-to-all-start.1 = ((bf16[8,128,1024]{2,1,0:T(8,128)(2,1)}), bf16[8,128,1024]{2,1,0:T(8,128)(2,1)S(1)}, u32[]{:S(2)}, u32[]{:S(2)}) async-start(bf16[8,128,1024]{2,1,0:T(8,128)(2,1)} %bitcast.102), calls=%async_computation.1 | async-start | bytes 4194304 | tf_op jit(solution)/shard_map/all_to_all | solution.py:28
  125.6 81.3 %copy-start.5 = (f32[1024]{0:T(1024)S(1)}, f32[1024]{0:T(1024)}, u32[]{:S(2)}) copy-start(f32[1024]{0:T(1024)} %param.24) | copy-start | bytes 12292
  162.6 50.5 %all-to-all-start = ((s32[32,8,1]{1,2,0:T(1,128)}), s32[32,8,1]{1,2,0:T(1,128)S(1)}, u32[]{:S(2)}, u32[]{:S(2)}) async-start(s32[32,8,1]{1,2,0:T(1,128)} %bitcast), calls=%async_computation | async-start | bytes 32768 | tf_op jit(solution)/shard_map/all_to_all | solution.py:125
  206.4 11.6 %copy-start.7 = (bf16[1,8,24]{2,1,0:T(8,128)(2,1)S(1)}, bf16[1,8,24]{2,1,0:T(8,128)(2,1)}, u32[]{:S(2)}) copy-start(bf16[1,8,24]{2,1,0:T(8,128)(2,1)} %param.29) | copy-start | bytes 1156
  206.8 66.9 %copy-start.9 = (bf16[512,1024]{1,0:T(8,128)(2,1)S(1)}, bf16[512,1024]{1,0:T(8,128)(2,1)}, u32[]{:S(2)}) copy-start(bf16[512,1024]{1,0:T(8,128)(2,1)} %param.26) | copy-start | bytes 3145732
  213.1 60.7 %all-to-all-start.2 = ((bf16[32,8,1024]{2,1,0:T(8,128)(2,1)}), bf16[32,8,1024]{2,1,0:T(8,128)(2,1)S(1)}, u32[]{:S(2)}, u32[]{:S(2)}) async-start(bf16[32,8,1024]{2,1,0:T(8,128)(2,1)} %fusion.32), calls=%async_computation.2 | async-start | bytes 1048576 | tf_op jit(solution)/shard_map/all_to_all | solution.py:124
  218.0 235.2 %reduce-scatter.2.cloned.1.call-start = ((), (), s32[]{:S(2)}) async-start(), calls=%async_computation.6 | async-start | bytes 7077888 | tf_op jit(solution)/shard_map/reduce_scatter | solution.py:184
  273.3 21.7 %copy-start.12 = (f32[1024]{0:T(1024)S(1)}, f32[1024]{0:T(1024)}, u32[]{:S(2)}) copy-start(f32[1024]{0:T(1024)} %param.27) | copy-start | bytes 12292
  306.5 0.7 copy-start.4
  307.2 12.4 %collective-permute-start.4 = (s32[512]{0:T(512)S(1)}, s32[512]{0:T(512)S(1)}, u32[]{:S(2)}, u32[]{:S(2)}) collective-permute-start(s32[512]{0:T(512)S(1)} %copy-done.4), channel_id=1, source_target_pairs={{0,8},{8,16},{16,24},{24,32},{32,40},{40,48},{48,56},{56,64},{64,7... | collective-permute-start | bytes 6152 | tf_op jit(solution)/shard_map/ppermute | solution.py:35
  311.3 8.3 %collective-permute-start.5 = (s32[512]{0:T(512)S(1)}, s32[512]{0:T(512)S(1)}, u32[]{:S(2)}, u32[]{:S(2)}) collective-permute-start(s32[512]{0:T(512)S(1)} %copy-done.4), channel_id=1, source_target_pairs={{0,16},{8,24},{16,32},{24,40},{32,48},{40,56},{48,64},{56,72},{64,... | collective-permute-start | bytes 6152 | tf_op jit(solution)/shard_map/ppermute | solution.py:35
  313.3 6.4 %collective-permute-start.6 = (s32[512]{0:T(512)S(1)}, s32[512]{0:T(512)S(1)}, u32[]{:S(2)}, u32[]{:S(2)}) collective-permute-start(s32[512]{0:T(512)S(1)} %copy-done.4), channel_id=1, source_target_pairs={{0,24},{8,32},{16,40},{24,48},{32,56},{40,64},{48,72},{56,80},{64,... | collective-permute-start | bytes 6152 | tf_op jit(solution)/shard_map/ppermute | solution.py:35
  315.2 4.5 collective-permute-start.7
  316.8 2.7 copy-start.6
  456.6 59.0 %collective-permute-start = (bf16[512,1,128]{2,0,1:T(8,128)(2,1)}, bf16[512,1,128]{2,0,1:T(8,128)(2,1)S(1)}, u32[]{:S(2)}, u32[]{:S(2)}) collective-permute-start(bf16[512,1,128]{2,0,1:T(8,128)(2,1)} %get-tuple-element.6), channel_id=1, source_target_pairs={{0,8},{8,16},{16,24},{24,32},{32,40},{40,48},{48,56},{56,64},{64,7... | collective-permute-start | bytes 393224 | tf_op jit(solution)/shard_map/ppermute | solution.py:35
  466.5 49.1 %collective-permute-start.1 = (bf16[512,1,128]{2,0,1:T(8,128)(2,1)}, bf16[512,1,128]{2,0,1:T(8,128)(2,1)S(1)}, u32[]{:S(2)}, u32[]{:S(2)}) collective-permute-start(bf16[512,1,128]{2,0,1:T(8,128)(2,1)} %get-tuple-element.6), channel_id=1, source_target_pairs={{0,16},{8,24},{16,32},{24,40},{32,48},{40,56},{48,64},{56,72},{64,... | collective-permute-start | bytes 393224 | tf_op jit(solution)/shard_map/ppermute | solution.py:35
  469.3 46.3 %collective-permute-start.2 = (bf16[512,1,128]{2,0,1:T(8,128)(2,1)}, bf16[512,1,128]{2,0,1:T(8,128)(2,1)S(1)}, u32[]{:S(2)}, u32[]{:S(2)}) collective-permute-start(bf16[512,1,128]{2,0,1:T(8,128)(2,1)} %get-tuple-element.6), channel_id=1, source_target_pairs={{0,24},{8,32},{16,40},{24,48},{32,56},{40,64},{48,72},{56,80},{64,... | collective-permute-start | bytes 393224 | tf_op jit(solution)/shard_map/ppermute | solution.py:35
  473.3 14.6 %collective-permute-start.8 = (bf16[512,1,128]{2,0,1:T(8,128)(2,1)}, bf16[512,1,128]{2,0,1:T(8,128)(2,1)}, u32[]{:S(2)}, u32[]{:S(2)}) collective-permute-start(bf16[512,1,128]{2,0,1:T(8,128)(2,1)} %get-tuple-element.10), channel_id=1, source_target_pairs={{0,8},{8,16},{16,24},{24,32},{32,40},{40,48},{48,56},{56,64},{64,7... | collective-permute-start | bytes 393224 | tf_op jit(solution)/shard_map/ppermute | solution.py:35
  476.7 16.4 %collective-permute-start.9 = (bf16[512,1,128]{2,0,1:T(8,128)(2,1)}, bf16[512,1,128]{2,0,1:T(8,128)(2,1)}, u32[]{:S(2)}, u32[]{:S(2)}) collective-permute-start(bf16[512,1,128]{2,0,1:T(8,128)(2,1)} %get-tuple-element.10), channel_id=1, source_target_pairs={{0,16},{8,24},{16,32},{24,40},{32,48},{40,56},{48,64},{56,72},{64,... | collective-permute-start | bytes 393224 | tf_op jit(solution)/shard_map/ppermute | solution.py:35
  482.0 4.3 copy-start
  487.7 15.2 %copy-start.2 = (pred[512,2560]{0,1:T(8,128)(4,1)S(1)}, pred[512,2560]{0,1:T(8,128)(4,1)}, u32[]{:S(2)}) copy-start(pred[512,2560]{0,1:T(8,128)(4,1)} %and_and_fusion) | copy-start | bytes 3932164
  487.9 9.1 %collective-permute-start.10 = (bf16[512,1,128]{2,0,1:T(8,128)(2,1)}, bf16[512,1,128]{2,0,1:T(8,128)(2,1)S(1)}, u32[]{:S(2)}, u32[]{:S(2)}) collective-permute-start(bf16[512,1,128]{2,0,1:T(8,128)(2,1)} %get-tuple-element.10), channel_id=1, source_target_pairs={{0,24},{8,32},{16,40},{24,48},{32,56},{40,64},{48,72},{56,80},{64,... | collective-permute-start | bytes 393224 | tf_op jit(solution)/shard_map/ppermute | solution.py:35
  493.1 9.2 %collective-permute-start.11 = (bf16[512,1,128]{2,0,1:T(8,128)(2,1)}, bf16[512,1,128]{2,0,1:T(8,128)(2,1)S(1)}, u32[]{:S(2)}, u32[]{:S(2)}) collective-permute-start(bf16[512,1,128]{2,0,1:T(8,128)(2,1)} %get-tuple-element.10), channel_id=1, source_target_pairs={{0,32},{8,40},{16,48},{24,56},{32,64},{40,72},{48,80},{56,88},{64,... | collective-permute-start | bytes 393224 | tf_op jit(solution)/shard_map/ppermute | solution.py:35
  497.0 18.7 %collective-permute-start.3 = (bf16[512,1,128]{2,0,1:T(8,128)(2,1)}, bf16[512,1,128]{2,0,1:T(8,128)(2,1)S(1)}, u32[]{:S(2)}, u32[]{:S(2)}) collective-permute-start(bf16[512,1,128]{2,0,1:T(8,128)(2,1)} %get-tuple-element.6), channel_id=1, source_target_pairs={{0,32},{8,40},{16,48},{24,56},{32,64},{40,72},{48,80},{56,88},{64,... | collective-permute-start | bytes 393224 | tf_op jit(solution)/shard_map/ppermute | solution.py:35
  503.0 12.6 %copy-start.3 = (bf16[2560,1,128]{2,0,1:T(8,128)(2,1)S(1)}, bf16[2560,1,128]{2,0,1:T(8,128)(2,1)}, u32[]{:S(2)}) copy-start(bf16[2560,1,128]{2,0,1:T(8,128)(2,1)} %get-tuple-element.5) | copy-start | bytes 1966084
Sparse Core Ops, SparseCore 0:
  9.1 98.8 all-gather.2
  109.8 131.6 all-gather.4
  306.7 146.5 reduce-scatter.1
where the time goes:
time: 534 us; the launch traced here: 532 us
  waiting for transfers between devices  224 us (42%)
  blocking collectives  116 us (22%)
  starting transfers between devices  98.7 us (18%)
  matrix products  40.8 us (8%)
  other arithmetic  21.9 us (4%)
  local copies, waits for them, and re-layouts  16.3 us (3%)
  between operations  14.4 us (3%)
    reduce_scatter x1, waiting for transfers between devices, on_device(): lax.psum_scatter(partial_value.astype(jnp.bfloat16), 'wt', scatter_dimens...  130 us
    all_gather x1, blocking collectives, on_device(): lax.all_gather(llm_scales, 'ctx', axis=2, tiled=True)  54.7 us
    all_gather x1, waiting for transfers between devices, merge_project(): codes_piece = lax.all_gather(merger_codes, 'ctx', axis=2, tiled=True)  51.3 us
    all_to_all x1, starting transfers between devices, route_tokens(): lax.all_to_all(labels, 'ctx', split_axis=0, concat_axis=0, tiled=True)  43.8 us
    ppermute x12, starting transfers between devices, passed_along(): lax.ppermute(value, axis, [(source, source + steps) for source in range(l...  41.9 us
    all_gather x1, blocking collectives, merge_project(): scale_piece = lax.all_gather(merger_scales, 'ctx', axis=2, tiled=True)  40.4 us
    all_to_all x1, waiting for transfers between devices, summed_on_arrival(): lax.all_to_all(parts, axis, split_axis=0, concat_axis=0, tiled=True)  36 us
    psum x1, blocking collectives, on_device(): squares = lax.psum(jnp.sum(values * values, axis=1), 'wt')  20.6 us
  transfers between devices with their start and end apart: 18, of which 4 were waited for; matrix products, arithmetic and copies ran while one was open for 10% of the time, Pallas kernels for 0%

commit v1 on v0

v1 whole, which is shorter than its diff:
```python
import functools

import jax
import jax.numpy as jnp
from jax import lax
from jax.experimental import pallas as pl
from jax.experimental.pallas import tpu as pltpu
from jax.sharding import PartitionSpec as P

VHD = 80
D = 8192
KVH = 8
HD = 128
GROUP = 4
MERGE = 4
REACH = 4
CAP = 8

VIT_EPS = 1e-06
RMS_EPS = 1e-06
ROPE_BASE = 1000000.0
FILL_LOW = -1e30

NX = 4
NZ = 4
NY = 4
BF = jnp.bfloat16
F32 = jnp.float32


def here():
    c = lax.axis_index("ctx")
    w = lax.axis_index("wt")
    return {"z": c // 8, "x": (c // 2) % 4, "k": c % 2, "y": w // 2, "h": w % 2}


def device_of(at):
    return {"ctx": at["z"] * 8 + at["x"] * 2 + at["k"], "wt": at["y"] * 2 + at["h"]}


SIZES = {"z": 4, "x": 4, "k": 2, "y": 4, "h": 2}


def moved(at, **offsets):
    new = dict(at)
    for name, offset in offsets.items():
        new[name] = (at[name] + offset) % SIZES[name]
    return new


class Net:
    def __init__(self, send_sems, recv_sems, local_sems):
        self.send_sems, self.recv_sems, self.local_sems = send_sems, recv_sems, local_sems
        self.sent, self.kept = [], []

    def send(self, src, dst, to):
        i = len(self.sent)
        copy = pltpu.make_async_remote_copy(
            src_ref=src,
            dst_ref=dst,
            send_sem=self.send_sems.at[i],
            recv_sem=self.recv_sems.at[i],
            device_id=device_of(to),
            device_id_type=pl.DeviceIdType.MESH,
        )
        copy.start()
        self.sent.append([copy, False])
        return i

    def local(self, src, dst):
        copy = pltpu.make_async_copy(src, dst, self.local_sems.at[len(self.kept)])
        copy.start()
        self.kept.append(copy)

    def arrived(self, i):
        if not self.sent[i][1]:
            self.sent[i][0].wait_recv()
            self.sent[i][1] = True

    def finish(self):
        for copy in self.kept:
            copy.wait()
        for i in range(len(self.sent)):
            self.arrived(i)
        for copy, _ in self.sent:
            copy.wait_send()


def greet(peers):
    barrier = pltpu.get_barrier_semaphore()
    for peer in peers:
        pl.semaphore_signal(
            barrier, inc=1, device_id=device_of(peer), device_id_type=pl.DeviceIdType.MESH
        )
    pl.semaphore_wait(barrier, len(peers))


def exchange(name, cid, body, peers, in_spaces, ins, outs, aliases, sends, locals_=1):
    def kernel(*refs):
        in_refs = refs[: len(ins)]
        out_refs = refs[len(ins) : len(ins) + len(outs)]
        send_sems, recv_sems, local_sems = refs[len(ins) + len(outs) :]
        at = here()
        greet(peers(at))
        net = Net(send_sems, recv_sems, local_sems)
        body(at, net, in_refs, out_refs)
        net.finish()

    return pl.pallas_call(
        kernel,
        out_shape=outs,
        in_specs=[pl.BlockSpec(memory_space=s) for s in in_spaces],
        out_specs=[pl.BlockSpec(memory_space=pltpu.HBM) for _ in outs],
        scratch_shapes=[
            pltpu.SemaphoreType.DMA((sends,)),
            pltpu.SemaphoreType.DMA((sends,)),
            pltpu.SemaphoreType.DMA((max(1, locals_),)),
        ],
        input_output_aliases=aliases,
        compiler_params=pltpu.CompilerParams(collective_id=cid, has_side_effects=True),
        name=name,
    )(*ins)


V = pltpu.VMEM
H = pltpu.HBM
LEFT = (1, 2, 3)
T1, T2 = 256, 384


def spread(features, places, merger_piece, llm_piece, bias_rows, text):
    tokens, depth = features.shape
    cols = merger_piece.shape[0]
    heads2, wide, rows = llm_piece.shape[1:]

    def peers(at):
        return (
            [moved(at, z=d) for d in LEFT]
            + [moved(at, x=d) for d in LEFT]
            + [moved(at, y=d) for d in LEFT]
            + [moved(at, k=1)]
        )

    def body(at, net, i, o):
        feat, place, merger, llm, bias, txt = i
        feat_all, place_all, merger_all, bias_all, llm_all, txt_all = o
        z, x, k, y = at["z"], at["x"], at["k"], at["y"]
        mine = x * 2 + k
        passing = []
        for d in LEFT:
            net.send(feat, feat_all.at[z], moved(at, z=d))
            net.send(place, place_all.at[z], moved(at, z=d))
            passing.append(net.send(merger, merger_all.at[mine], moved(at, x=d)))
            to = moved(at, y=d)
            net.send(llm.at[to["y"]], llm_all.at[y, :, z, x, k], to)
            net.send(bias, bias_all.at[y], to)
        net.send(merger, merger_all.at[mine], moved(at, k=1))
        for d in LEFT:
            net.send(txt.at[:T1], txt_all.at[y, :T1], moved(at, y=d))
        net.local(feat, feat_all.at[z])
        net.local(place, place_all.at[z])
        net.local(merger, merger_all.at[mine])
        net.local(llm.at[y], llm_all.at[y, :, z, x, k])
        net.local(bias, bias_all.at[y])
        net.local(txt, txt_all.at[y])
        for d, n in zip(LEFT, passing):
            net.arrived(n)
            source = ((x + 4 - d) % 4) * 2 + k
            net.send(merger_all.at[source], merger_all.at[source], moved(at, k=1))

    sds = jax.ShapeDtypeStruct
    return exchange(
        "spread",
        1,
        body,
        peers,
        [V] * 6,
        (features, places, merger_piece, llm_piece, bias_rows, text),
        (
            sds((NZ, tokens, depth), BF),
            sds((NZ,) + places.shape, jnp.int32),
            sds((NX * 2, cols, depth), BF),
            sds((NY,) + bias_rows.shape, F32),
            sds((NY, heads2, NZ, NX, 2, wide, rows), BF),
            sds((NY,) + text.shape, BF),
        ),
        {},
        15 + 1 + 3 + 3,
        6,
    )


def reduce_y(partial, llm_all):
    def peers(at):
        return [moved(at, y=d) for d in LEFT] + [moved(at, z=d) for d in LEFT]

    def body(at, net, i, o):
        part, _ = i
        got, llm = o
        z, x, k = at["z"], at["x"], at["k"]
        for d in LEFT:
            to = moved(at, y=d)
            net.send(part.at[to["y"]], got.at[d - 1], to)
        for d in LEFT:
            net.send(llm.at[:, :, z, x, k], llm.at[:, :, z, x, k], moved(at, z=d))

    sds = jax.ShapeDtypeStruct
    return exchange(
        "reduce_y",
        2,
        body,
        peers,
        [V, H],
        (partial, llm_all),
        (sds((3,) + partial.shape[1:], BF), sds(llm_all.shape, BF)),
        {1: 1},
        6,
    )


def reduce_h(half, llm_all, text, txt_all):
    def peers(at):
        return (
            [moved(at, h=1)]
            + [moved(at, x=d) for d in (1, 3)]
            + [moved(at, y=d) for d in LEFT]
        )

    def body(at, net, i, o):
        part, _, txt, _ = i
        got, llm, txt_all_ = o
        x, k, y = at["x"], at["k"], at["y"]
        net.send(part, got, moved(at, h=1))
        for d in (1, 3):
            piece = llm.at[:, :, pl.ds(0, 2), x, k]
            net.send(piece, piece, moved(at, x=d))
        for d in LEFT:
            net.send(txt.at[T1:T2], txt_all_.at[y, T1:T2], moved(at, y=d))

    sds = jax.ShapeDtypeStruct
    return exchange(
        "reduce_h",
        3,
        body,
        peers,
        [V, H, V, H],
        (half, llm_all, text, txt_all),
        (sds(half.shape, BF), sds(llm_all.shape, BF), sds(txt_all.shape, BF)),
        {1: 1, 3: 2},
        6,
    )


OTHERS = [(a, b, e) for a in range(4) for b in range(4) for e in range(2) if (a, b, e) != (0, 0, 0)]


def route(packed, llm_all, text, txt_all):
    def peers(at):
        return [moved(at, z=a, x=b, k=e) for a, b, e in OTHERS] + [moved(at, y=d) for d in LEFT]

    def body(at, net, i, o):
        pack, _, txt, _ = i
        got, llm, txt_all_ = o
        z, x, k, y = at["z"], at["x"], at["k"], at["y"]
        mine = got.at[z, x * 2 + k]
        for a, b, e in OTHERS:
            to = moved(at, z=a, x=b, k=e)
            net.send(pack.at[to["z"] * 8 + to["x"] * 2 + to["k"]], mine, to)
        for d in (1, 3):
            piece = llm.at[:, :, pl.ds(2, 2), x, k]
            net.send(piece, piece, moved(at, x=d))
        for d in LEFT:
            net.send(txt.at[T2:], txt_all_.at[y, T2:], moved(at, y=d))
        net.local(pack.at[z * 8 + x * 2 + k], mine)

    sds = jax.ShapeDtypeStruct
    return exchange(
        "route",
        4,
        body,
        peers,
        [V, H, V, H],
        (packed, llm_all, text, txt_all),
        (
            sds((NZ, NX * 2) + packed.shape[1:], BF),
            sds(llm_all.shape, BF),
            sds(txt_all.shape, BF),
        ),
        {1: 1, 3: 2},
        len(OTHERS) + 5,
    )


def collect(image, llm_all):
    def peers(at):
        return (
            [moved(at, y=d) for d in LEFT] + [moved(at, x=d) for d in (1, 3)] + [moved(at, k=1)]
        )

    def body(at, net, i, o):
        img, _ = i
        got, llm = o
        x, k, y = at["x"], at["k"], at["y"]
        for d in LEFT:
            net.send(img, got.at[:, y], moved(at, y=d))
        far = []
        for d, first in ((1, 0), (3, 2)):
            piece = llm.at[:, :, pl.ds(first, 2), (x + 4 - d) % 4, k]
            far.append(net.send(piece, piece, moved(at, x=d)))
        for step in (0, 1, 3):
            piece = llm.at[:, :, :, (x + step) % 4, k]
            net.send(piece, piece, moved(at, k=1))
        net.local(img, got.at[:, y])
        for n, first in zip(far, (0, 2)):
            net.arrived(n)
            piece = llm.at[:, :, pl.ds(first, 2), (x + 2) % 4, k]
            net.send(piece, piece, moved(at, k=1))

    sds = jax.ShapeDtypeStruct
    return exchange(
        "collect",
        5,
        body,
        peers,
        [V, H],
        (image, llm_all),
        (sds((image.shape[0], NY) + image.shape[1:], BF), sds(llm_all.shape, BF)),
        {1: 1},
        3 + 2 + 3 + 2,
    )


def reduce_qkv(part, squares):
    def peers(at):
        return [moved(at, h=1)]

    def body(at, net, i, o):
        for src, dst in zip(i, o):
            net.send(src, dst, moved(at, h=1))

    sds = jax.ShapeDtypeStruct
    return exchange(
        "reduce_qkv",
        6,
        body,
        peers,
        [V, V],
        (part, squares),
        (sds(part.shape, BF), sds(squares.shape, F32)),
        {},
        2,
    )


def ahead(at, steps):
    place = (at["z"] * 8 + at["x"] * 2 + at["k"] + 32 + steps) % 32
    return {"z": place // 8, "x": (place // 2) % 4, "k": place % 2, "y": at["y"], "h": at["h"]}


def halo(kv, segs):
    def peers(at):
        return [ahead(at, s) for s in (1, 2, 3, 4, -1, -2, -3, -4)]

    def body(at, net, i, o):
        kv_in, seg_in = i
        kv_out, seg_out = o
        for s in range(1, REACH + 1):
            net.send(kv_in, kv_out.at[s], ahead(at, s))
            net.send(seg_in, seg_out.at[s], ahead(at, s))
        net.local(kv_in, kv_out.at[0])
        net.local(seg_in, seg_out.at[0])

    sds = jax.ShapeDtypeStruct
    return exchange(
        "halo",
        7,
        body,
        peers,
        [V, V],
        (kv, segs),
        (sds((REACH + 1,) + kv.shape, BF), sds((REACH + 1,) + segs.shape, jnp.int32)),
        {},
        2 * REACH,
        2,
    )


def softmax_rows(scores, allowed):
    masked = jnp.where(allowed, scores, FILL_LOW)
    highest = jnp.max(masked, axis=-1, keepdims=True)
    raised = jnp.exp(masked - highest)
    return raised / jnp.sum(raised, axis=-1, keepdims=True)


def vision_norm_rows(patches, vit_gain):
    values = patches.astype(F32)
    mean_square = jnp.mean(values * values, axis=1, keepdims=True)
    return (values * lax.rsqrt(mean_square + VIT_EPS) * vit_gain).astype(BF)


def window_attention(normed, weight_block, bias_block, window_ids):
    row_count = normed.shape[0]
    packed = jnp.dot(
        normed, weight_block.reshape(normed.shape[1], -1), preferred_element_type=F32
    )
    triple = (packed.reshape(row_count, 3, -1) + bias_block).astype(BF)
    heads_here = triple.shape[2] // VHD
    queries = triple[:, 0].reshape(row_count, heads_here, VHD)
    keys_here = triple[:, 1].reshape(row_count, heads_here, VHD)
    values_here = triple[:, 2].reshape(row_count, heads_here, VHD)
    scores = jnp.einsum(
        "qhd,khd->hqk", queries, keys_here, preferred_element_type=F32
    ) * VHD ** (-0.5)
    allowed = window_ids[:, None] == window_ids[None, :]
    softmaxed = softmax_rows(scores, allowed[None]).astype(BF)
    blended = jnp.einsum("hqk,khd->qhd", softmaxed, values_here, preferred_element_type=F32)
    return blended.astype(BF).reshape(row_count, -1)


def rope_tables(first, length):
    places = (first + jnp.arange(length, dtype=jnp.int32)).astype(F32)
    frequency = ROPE_BASE ** (-jnp.arange(0, HD, 2).astype(F32) / HD)
    angles = places[:, None] * frequency[None, :]
    angles = jnp.concatenate([angles, angles], axis=1)
    return (jnp.cos(angles), jnp.sin(angles))


def rotary(inputs, cosine, sine):
    halfway = inputs.shape[-1] // 2
    turned = jnp.concatenate([-inputs[..., halfway:], inputs[..., :halfway]], axis=-1)
    return inputs * cosine + turned * sine


def pack_tokens(values, positions, span, owners):
    items = values.shape[0]
    target = positions // span
    item_order = jnp.arange(items, dtype=jnp.int32)
    before = (target[None, :] == target[:, None]) & (item_order[None, :] < item_order[:, None])
    ranks = jnp.sum(before.astype(jnp.int32), axis=1)
    slots = target * CAP + ranks
    table = slots[None, :] == jnp.arange(owners * CAP, dtype=jnp.int32)[:, None]
    local = positions - target * span
    lanes = jnp.arange(HD)[None, :]
    notes = jnp.where(lanes == 0, (local // 16)[:, None], (local % 16)[:, None])
    notes = jnp.where(lanes == 2, 1, notes)
    rows = jnp.concatenate([values, notes.astype(BF)], axis=1)
    packed = jnp.dot(table.astype(BF), rows, preferred_element_type=F32).astype(BF)
    return packed.reshape(owners, CAP, rows.shape[1])


def project(hidden, weights):
    blocks = [
        lax.dot_general(
            hidden[b],
            weights[b],
            (((1,), (1,)), ((), ())),
            preferred_element_type=F32,
        )
        for b in range(hidden.shape[0])
    ]
    return (blocks[0] + blocks[1]) + (blocks[2] + blocks[3])


def on_device(
    patches,
    vit_gain,
    vit_codes,
    vit_scales,
    vit_bias,
    window_ids,
    merger_codes,
    merger_scales,
    merger_bias,
    positions,
    text_embed,
    norm_gain,
    llm_codes,
    llm_scales,
    llm_bias,
    segments,
):
    at = here()
    owners = lax.axis_size("ctx")
    row_count, width = text_embed.shape
    first = lax.axis_index("ctx") * row_count

    llm_weight = (llm_codes.astype(F32) * llm_scales.astype(F32)).astype(BF)
    llm_weight = (llm_weight.astype(F32) * norm_gain[:, None, None]).astype(BF)
    llm_piece = jnp.transpose(llm_weight, (1, 2, 0)).reshape(NY, 2, -1, width)
    merger_weight = (merger_codes.astype(F32) * merger_scales.astype(F32)).astype(BF)
    merger_piece = merger_weight.reshape(-1, merger_weight.shape[2]).T

    normed_patches = vision_norm_rows(patches, vit_gain)
    vit_weight = (vit_codes.astype(F32) * vit_scales.astype(F32)[0]).astype(BF)
    attended = window_attention(normed_patches, vit_weight, vit_bias, window_ids)
    token_count = positions.shape[0]
    features = attended.reshape(token_count, -1)
    place_rows = jnp.broadcast_to(positions[None, :], (8, token_count))

    feat_all, place_all, merger_all, bias_all, llm_all, txt_all = spread(
        features, place_rows, merger_piece, llm_piece, merger_bias.reshape(8, -1), text_embed
    )
    product = lax.dot_general(
        feat_all.reshape(-1, feat_all.shape[2]),
        merger_all.reshape(-1, merger_all.shape[2]),
        (((1,), (1,)), ((), ())),
        preferred_element_type=F32,
    ).astype(BF)
    product = product.reshape(NZ, token_count, -1)
    got, llm_all = reduce_y(product, llm_all)
    total = lax.dynamic_index_in_dim(product, at["y"], 0, keepdims=False).astype(F32)
    total = total + got.astype(F32).sum(axis=0)
    low, high = (total[:, :width], total[:, width:])
    is_high = at["h"] == 1
    keep = jnp.where(is_high, high, low)
    give = jnp.where(is_high, low, high).astype(BF)
    got, llm_all, txt_all = reduce_h(give, llm_all, text_embed, txt_all)
    bias_here = lax.dynamic_index_in_dim(bias_all, at["z"], 0, keepdims=False).reshape(-1)
    merged = (keep + got.astype(F32) + bias_here).astype(BF)
    places_here = lax.dynamic_index_in_dim(place_all, at["y"], 0, keepdims=False)[0]
    packed = pack_tokens(merged, places_here, row_count, owners)
    image, llm_all, txt_all = route(packed, llm_all, text_embed, txt_all)
    image = image.reshape(NZ, -1, image.shape[3])
    slots, llm_all = collect(image, llm_all)
    slots = slots.reshape(NZ, -1, slots.shape[3])

    notes = slots[0, :, width : width + 3].astype(F32)
    local = jnp.where(notes[:, 2] > 0.5, notes[:, 0] * 16.0 + notes[:, 1], -1.0).astype(jnp.int32)
    table = local[None, :] == jnp.arange(row_count, dtype=jnp.int32)[:, None]
    filled = jnp.stack(
        [
            jnp.dot(table.astype(BF), slots[b, :, :width], preferred_element_type=F32).astype(BF)
            for b in range(NY)
        ]
    )
    covered = jnp.any(table, axis=1)
    hidden = jnp.where(covered[None, :, None], filled, txt_all)
    raised = hidden.astype(F32)
    squares = jnp.sum(raised * raised, axis=(0, 2))
    weights = llm_all.reshape(NY, -1, width)
    partial_sum = project(hidden, weights)
    columns = partial_sum.shape[1] // 2
    low, high = (partial_sum[:, :columns], partial_sum[:, columns:])
    keep = jnp.where(is_high, high, low)
    give = jnp.where(is_high, low, high).astype(BF)
    square_rows = squares.reshape(-1, 128)
    got, got_squares = reduce_qkv(give, square_rows)
    scale = lax.rsqrt((squares + got_squares.reshape(-1)) / D + RMS_EPS)
    triple = (keep + got.astype(F32)) * scale[:, None] + llm_bias

    cosine, sine = rope_tables(first, row_count)
    queries = rotary(
        triple[:, : GROUP * HD].reshape(row_count, GROUP, HD), cosine[:, None], sine[:, None]
    ).astype(BF)
    keys_rot = rotary(triple[:, GROUP * HD : (GROUP + 1) * HD], cosine, sine).astype(BF)
    values_cut = triple[:, (GROUP + 1) * HD :].astype(BF)
    kv_all, seg_all = halo(
        jnp.concatenate([keys_rot, values_cut], axis=1), segments.reshape(-1, 128)
    )
    keys_all = kv_all[:, :, :HD].reshape(-1, HD)
    values_all = kv_all[:, :, HD:].reshape(-1, HD)
    key_segments = seg_all.reshape(-1)
    key_places = jnp.concatenate(
        [
            first - distance * row_count + jnp.arange(row_count, dtype=jnp.int32)
            for distance in range(REACH + 1)
        ],
        axis=0,
    )
    query_places = first + jnp.arange(row_count, dtype=jnp.int32)
    allowed = (
        (segments[:, None] == key_segments[None, :])
        & (key_places[None, :] <= query_places[:, None])
        & (key_places[None, :] >= 0)
    )
    scores = jnp.einsum(
        "qjd,kd->jqk", queries, keys_all, preferred_element_type=F32
    ) * HD ** (-0.5)
    softmaxed = softmax_rows(scores, allowed[None]).astype(BF)
    blended = jnp.einsum("jqk,kd->qjd", softmaxed, values_all, preferred_element_type=F32)
    return blended.astype(BF).reshape(row_count, -1)


def solution(mesh):
    in_specs = (
        P("ctx", None),
        P(),
        P(None, None, "wt"),
        P("wt"),
        P(None, "wt"),
        P("ctx"),
        P(None, "wt", "ctx"),
        P(None, "wt", "ctx"),
        P("wt"),
        P("ctx"),
        P("ctx", "wt"),
        P("wt"),
        P("wt", None, "ctx"),
        P("wt", None, "ctx"),
        P("wt", None),
        P("ctx"),
    )
    out_specs = P("ctx", "wt")
    return jax.shard_map(
        on_device, mesh=mesh, in_specs=in_specs, out_specs=out_specs, check_vma=False
    )
```

time: 534 us -> 329 us (0.62)
  Pallas kernels: 0 us -> 239 us
  waiting for transfers between devices: 224 us -> 0 us
  blocking collectives: 116 us -> 0 us
  starting transfers between devices: 98.7 us -> 0 us
  between operations: 14.4 us -> 1.22 us
  matrix products: 40.8 us -> 48.1 us
    pallas_call x0 -> x7, Pallas kernels: none -> 239 us  [exchange(): pl.pallas_call(kernel, out_shape=outs, in_specs=[pl.BlockSpec(memory_spac...]
    reduce_scatter x1 -> x0, waiting for transfers between devices: 130 us -> none  [on_device(): lax.psum_scatter(partial_value.astype(jnp.bfloat16), 'wt', scatter_dimens...]
    all_gather x2 -> x0, blocking collectives: 95.1 us -> none  [the longest x1 54.7 us: on_device(): lax.all_gather(llm_scales, 'ctx', axis=2, tiled=True)]
    all_to_all x3 -> x0, starting transfers between devices: 56.7 us -> none  [the longest x1 43.8 us: route_tokens(): lax.all_to_all(labels, 'ctx', split_axis=0, concat_axis=0, tiled=True)]
    all_gather x2 -> x0, waiting for transfers between devices: 51.3 us -> none  [the longest x1 51.3 us: merge_project(): codes_piece = lax.all_gather(merger_codes, 'ctx', axis=2, tiled=True)]
    ppermute x12 -> x0, starting transfers between devices: 41.9 us -> none  [passed_along(): lax.ppermute(value, axis, [(source, source + steps) for source in range(l...]
    all_to_all x3 -> x0, waiting for transfers between devices: 41.2 us -> none  [the longest x1 36 us: summed_on_arrival(): lax.all_to_all(parts, axis, split_axis=0, concat_axis=0, tiled=True)]
    psum x1 -> x0, blocking collectives: 20.6 us -> none  [on_device(): squares = lax.psum(jnp.sum(values * values, axis=1), 'wt')]
  transfers between devices with their start and end apart: 18 -> 0, of which waited for: 4 -> 0; matrix products, arithmetic and copies ran while one was open for 10% -> 0% of each run, Pallas kernels for 0% -> 0%
where the time goes in v1:
time: 329 us; the launch traced here: 328 us
  Pallas kernels  239 us (73%)
  matrix products  48.1 us (15%)
  other arithmetic  22.5 us (7%)
  local copies, waits for them, and re-layouts  17.1 us (5%)
    pallas_call x7, Pallas kernels, exchange(): pl.pallas_call(kernel, out_shape=outs, in_specs=[pl.BlockSpec(memory_spac...  239 us
    sub x2, matrix products, softmax_rows(): raised = jnp.exp(masked - highest)  13.8 us
    dot_general x4, matrix products, project(): lax.dot_general(hidden[b], weights[b], (((1,), (1,)), ((), ())), preferre...  9.34 us
    dot_general x1, matrix products, on_device(): jnp.einsum('jqk,kd->qjd', softmaxed, values_all, preferred_element_type=F32)  8.74 us

profile of v1, /device:TPU:3, one launch (start us, length us, event | category | flops | bytes accessed | tf_op | source)
XLA Modules:
  0.0 327.8 jit_solution(16820758984198117837)
XLA Ops:
  0.0 1.6 fusion.8
  2.3 2.6 fusion.24
  5.2 1.0 fusion.83
  6.3 1.2 fusion.30
  7.7 0.9 reshape_reshape.3.refs_0_
  8.7 0.9 copy.40
  9.6 0.9 multiply_convert_fusion.1
  11.1 36.4 %spread.1 = (bf16[4,128,640]{2,1,0:T(8,128)(2,1)}, s32[4,8,128]{2,1,0:T(8,128)}, bf16[8,256,640]{2,1,0:T(8,128)(2,1)}, f32[4,8,128]{2,1,0:T(8,128)}, bf16[4,2,4,...) custom-call(bf16[128,640]{1,0:T(8,128)(2,1)} %reshape_reshape.3.refs_0_, ...), custom_call_target="tpu_custom_call" | custom-call | tf_op jit(solution)/shard_map/spread/pallas_call | solution.py:109
  47.5 5.1 %convolution_convert_fusion = bf16[512,2048]{1,0:T(8,128)(2,1)} fusion(bf16[512,640]{1,0:T(8,128)(2,1)} %bitcast.222, bf16[2048,640]{1,0:T(8,128)(2,1)} %bitcast.221), kind=kOutput, calls=%fused_computation.19 | convolution fusion | flops 1343225856 | bytes 5373952 | tf_op jit(solution)/shard_map/dot_general | solution.py:503
  52.6 29.7 %reduce_y.1 = (bf16[3,128,2048]{2,1,0:T(8,128)(2,1)}, bf16[4,2,4,4,2,24,1024]{6,5,4,3,2,1,0:T(8,128)(2,1)}) custom-call(bf16[4,128,2048]{2,1,0:T(8,128)(2,1)} %bitcast.188, bf16[4,2,4,4,2,24,1024]{6,5,4,3,2,1,0:T(8,128)(2,1)} %get-tuple-element.28.refs_1_), custom_call_target="tpu_custom_call", output_to_operand_aliasing={{1}: (1, {})} | custom-call | tf_op jit(solution)/shard_map/reduce_y/pallas_call | solution.py:109
  82.3 1.8 convert_reduce_fusion
  84.1 1.2 convert_add_fusion
  85.3 0.8 select_convert_fusion.1.refs_0_
  86.1 24.9 %reduce_h.1 = (bf16[128,1024]{1,0:T(8,128)(2,1)}, bf16[4,2,4,4,2,24,1024]{6,5,4,3,2,1,0:T(8,128)(2,1)}, bf16[4,512,1024]{2,1,0:T(8,128)(2,1)}) custom-call(bf16[128,1024]{1,0:T(8,128)(2,1)} %select_convert_fusion.1.refs_0_, bf16[4,2,4,4,2,24,1024]{6,5,4,3,2,1,0:T(8,128)(2,1)} %get-tuple-element.30.refs_1_, ...), custom_call_target="tpu_custom_call", output_to_operand_aliasing={{1}: (1, {}), {2}: (3, {})} | custom-call | tf_op jit(solution)/shard_map/reduce_h/pallas_call | solution.py:109
  111.1 0.7 dynamic-slice_bitcast_fusion
  111.8 1.0 add_convert_fusion
  112.8 0.7 constant_dynamic-slice_fusion
  113.7 1.1 fusion.11.refs_0_
  114.9 39.8 %route.1 = (bf16[4,8,8,1152]{3,2,1,0:T(8,128)(2,1)}, bf16[4,2,4,4,2,24,1024]{6,5,4,3,2,1,0:T(8,128)(2,1)}, bf16[4,512,1024]{2,1,0:T(8,128)(2,1)}) custom-call(bf16[32,8,1152]{2,1,0:T(8,128)(2,1)} %fusion.11.refs_0_, bf16[4,2,4,4,2,24,1024]{6,5,4,3,2,1,0:T(8,128)(2,1)} %get-tuple-element.34.refs_1_, ...), custom_call_target="tpu_custom_call", output_to_operand_aliasing={{1}: (1, {}), {2}: (3, {})} | custom-call | tf_op jit(solution)/shard_map/route/pallas_call | solution.py:109
  154.7 29.6 %collect.1 = (bf16[4,4,64,1152]{3,2,1,0:T(8,128)(2,1)}, bf16[4,2,4,4,2,24,1024]{6,5,4,3,2,1,0:T(8,128)(2,1)}) custom-call(bf16[4,64,1152]{2,1,0:T(8,128)(2,1)} %bitcast.205, bf16[4,2,4,4,2,24,1024]{6,5,4,3,2,1,0:T(8,128)(2,1)} %get-tuple-element.37.refs_1_), custom_call_target="tpu_custom_call", output_to_operand_aliasing={{1}: (1, {})} | custom-call | tf_op jit(solution)/shard_map/collect/pallas_call | solution.py:109
  184.3 0.8 slice.145
  185.3 1.5 fusion.15
  186.8 1.6 fusion.16
  188.4 1.5 fusion.17
  189.9 1.5 fusion.18
  191.6 3.0 multiply_reduce_fusion
  194.7 1.5 copy-done
  196.2 3.5 %fusion.80 = (bf16[1,2,4,4,2,24,1024]{6,5,4,3,2,1,0:T(8,128)(2,1)S(1)}, bf16[1,2,4,4,2,24,1024]{6,5,4,3,2,1,0:T(8,128)(2,1)}, bf16[1,2,4,4,2,24,1024]{6,5,4,3,2,...) fusion(bf16[4,2,4,4,2,24,1024]{6,5,4,3,2,1,0:T(8,128)(2,1)S(1)} %copy-done), kind=kLoop, calls=%fused_computation.153 | loop fusion | bytes 25165824 | tf_op jit(solution)/shard_map/slice | solution.py:455
  199.7 3.8 %fusion.32 = f32[512,1536]{1,0:T(8,128)S(1)} fusion(bf16[1536,1024]{1,0:T(8,128)(2,1)} %bitcast.192, bf16[4,512,1024]{2,1,0:T(8,128)(2,1)S(1)} %get-tuple-element.46), kind=kOutput, calls=%fused_computation.57 | convolution fusion | flops 1610612736 | bytes 7340032 | tf_op jit(solution)/shard_map/dot_general | solution.py:453
  203.5 1.8 fusion.33
  205.3 1.9 convolution_add_fusion.1
  207.2 1.9 fusion.7
  209.1 1.0 select_convert_fusion.refs_0_
  210.1 40.6 %reduce_qkv.1 = (bf16[512,768]{1,0:T(8,128)(2,1)}, f32[4,128]{1,0:T(4,128)}) custom-call(bf16[512,768]{1,0:T(8,128)(2,1)} %select_convert_fusion.refs_0_, f32[4,128]{1,0:T(4,128)} %bitcast.217), custom_call_target="tpu_custom_call" | custom-call | tf_op jit(solution)/shard_map/reduce_qkv/pallas_call | solution.py:109
  251.5 1.4 multiply_add_fusion
  252.9 1.1 copy-done.2
  254.6 1.9 slice_negate_fusion
  256.8 1.2 fusion.62
  258.0 1.6 maximum_multiply_fusion
  259.7 0.7 pad_maximum_fusion.1.refs_0_
  260.4 37.8 %halo.1 = (bf16[5,512,256]{2,1,0:T(8,128)(2,1)}, s32[5,4,128]{2,1,0:T(4,128)}) custom-call(bf16[512,256]{1,0:T(8,128)(2,1)} %pad_maximum_fusion.1.refs_0_, s32[4,128]{1,0:T(4,128)} %bitcast.218), custom_call_target="tpu_custom_call" | custom-call | tf_op jit(solution)/shard_map/halo/pallas_call | solution.py:109
  298.2 0.7 eq.119
  299.0 2.5 and_and_fusion
  301.6 2.5 fusion.81
  304.0 1.2 mul.212
  305.2 12.8 %fusion.84 = (f32[4,512]{1,0:T(4,128)S(1)}, f32[4,512,2560]{1,2,0:T(8,128)}) fusion(pred[512,2560]{0,1:T(8,128)(4,1)S(1)} %and_and_fusion, bf16[2560,128,1]{1,0,2:T(8,128)(2,1)} %bitcast.204, f32[64,8,4,128]{3,2,1,0:T(4,128)} %bitcast.202, f32[64,8,4,128]{3,2,1,0:T(4,128)} %bitcast.201, f32[512,768]{1,0:T(8,128)S(1)} %copy-done.3), kind=kOutput, calls=%fused_computation.157 | convolution fusion | flops 1363937792 | bytes 26091520 | tf_op jit(solution)/shard_map/sub | solution.py:391
  318.0 8.7 %fusion.23 = bf16[128,4,512]{2,0,1:T(8,128)(2,1)S(1)} fusion(bf16[2560,128,1]{1,0,2:T(8,128)(2,1)} %bitcast.203, f32[4,512,2560]{1,2,0:T(8,128)} %get-tuple-element.67, f32[4,512]{1,0:T(4,128)S(1)} %get-tuple-element.66), kind=kOutput, calls=%fused_computation.45 | convolution fusion | flops 1352925184 | bytes 22159360 | tf_op jit(solution)/shard_map/jqk,kd->qjd/dot_general | solution.py:580
  326.8 1.0 copy.45
  (64 shorter events, 3.2 us)
Async XLA Ops:
  2.3 2.7 copy-start.9
  6.2 2.4 copy-start.14
  6.2 2.4 copy-start.7
  6.3 3.3 %copy-start.13 = (bf16[1,8,24]{2,1,0:T(8,128)(2,1)S(1)}, bf16[1,8,24]{2,1,0:T(8,128)(2,1)}, u32[]{:S(2)}) copy-start(bf16[1,8,24]{2,1,0:T(8,128)(2,1)} %param.29) | copy-start | bytes 1156
  6.3 3.3 %copy-start.6 = (bf16[1024,8,24]{0,2,1:T(8,128)(2,1)S(1)}, bf16[1024,8,24]{0,2,1:T(8,128)(2,1)}, u32[]{:S(2)}) copy-start(bf16[1024,8,24]{0,2,1:T(8,128)(2,1)} %param.28) | copy-start | bytes 1179652
  6.3 3.3 %copy-start.11 = (f32[1024]{0:T(1024)S(1)}, f32[1024]{0:T(1024)}, u32[]{:S(2)}) copy-start(f32[1024]{0:T(1024)} %param.27) | copy-start | bytes 12292
  7.5 3.0 copy-start.15
  186.8 4.8 %copy-start.1 = (bf16[4,512,1024]{2,1,0:T(8,128)(2,1)S(1)}, bf16[4,512,1024]{2,1,0:T(8,128)(2,1)}, u32[]{:S(2)}) copy-start(bf16[4,512,1024]{2,1,0:T(8,128)(2,1)} %get-tuple-element.39) | copy-start | bytes 12582916
  191.6 4.6 %copy-start = (bf16[4,2,4,4,2,24,1024]{6,5,4,3,2,1,0:T(8,128)(2,1)S(1)}, bf16[4,2,4,4,2,24,1024]{6,5,4,3,2,1,0:T(8,128)(2,1)}, u32[]{:S(2)}) copy-start(bf16[4,2,4,4,2,24,1024]{6,5,4,3,2,1,0:T(8,128)(2,1)} %get-tuple-element.40) | copy-start | bytes 37748740
  209.1 41.7 %copy-start.8 = (f32[512]{0:T(512)S(1)}, f32[512]{0:T(512)}, u32[]{:S(2)}) copy-start(f32[512]{0:T(512)} %get-tuple-element.45) | copy-start | bytes 6148
  209.1 42.3 %copy-start.12 = (f32[1,768]{1,0:T(1,128)S(1)}, f32[1,768]{1,0:T(1,128)}, u32[]{:S(2)}) copy-start(f32[1,768]{1,0:T(1,128)} %param.30) | copy-start | bytes 9220
  252.9 1.2 copy-start.2
  254.5 1.9 copy-start.3
  256.5 1.5 copy-start.4
  256.6 1.4 copy-start.5
  258.0 41.0 %copy-start.10 = (s32[512]{0:T(512)S(1)}, s32[512]{0:T(512)}, u32[]{:S(2)}) copy-start(s32[512]{0:T(512)} %param.31) | copy-start | bytes 6148

commit v2 on v1

--- a/solution.py
+++ b/solution.py
@@ -330,59 +330,256 @@
     )
 
 
-def reduce_qkv(part, squares):
-    def peers(at):
-        return [moved(at, h=1)]
-
-    def body(at, net, i, o):
-        for src, dst in zip(i, o):
-            net.send(src, dst, moved(at, h=1))
-
-    sds = jax.ShapeDtypeStruct
-    return exchange(
-        "reduce_qkv",
-        6,
-        body,
-        peers,
-        [V, V],
-        (part, squares),
-        (sds(part.shape, BF), sds(squares.shape, F32)),
-        {},
-        2,
-    )
-
-
 def ahead(at, steps):
     place = (at["z"] * 8 + at["x"] * 2 + at["k"] + 32 + steps) % 32
     return {"z": place // 8, "x": (place // 2) % 4, "k": place % 2, "y": at["y"], "h": at["h"]}
 
 
-def halo(kv, segs):
-    def peers(at):
-        return [ahead(at, s) for s in (1, 2, 3, 4, -1, -2, -3, -4)]
-
-    def body(at, net, i, o):
-        kv_in, seg_in = i
-        kv_out, seg_out = o
-        for s in range(1, REACH + 1):
-            net.send(kv_in, kv_out.at[s], ahead(at, s))
-            net.send(seg_in, seg_out.at[s], ahead(at, s))
-        net.local(kv_in, kv_out.at[0])
-        net.local(seg_in, seg_out.at[0])
-
-    sds = jax.ShapeDtypeStruct
-    return exchange(
-        "halo",
-        7,
-        body,
-        peers,
-        [V, V],
-        (kv, segs),
-        (sds((REACH + 1,) + kv.shape, BF), sds((REACH + 1,) + segs.shape, jnp.int32)),
-        {},
-        2 * REACH,
-        2,
-    )
+NEG = -1e30
+QT = 128
+
+
+def finish(slots, txt_all, weights, table, covered, bias, cosine, sine, seg_col, seg_row):
+    blocks, tokens, width = txt_all.shape
+    count = slots.shape[1]
+    columns = weights.shape[2]
+    qcols = GROUP * HD
+    kvcols = 2 * HD
+
+    def kernel(
+        slots_h,
+        txt_h,
+        w_h,
+        table_ref,
+        cov_ref,
+        bias_ref,
+        cos_ref,
+        sin_ref,
+        segc_ref,
+        segr_ref,
+        out_ref,
+        slots_v,
+        hid,
+        w_v,
+        sq,
+        sq_send,
+        sq_got,
+        kv_keep,
+        kv_send,
+        kv_got,
+        q_keep,
+        q_send,
+        q_got,
+        q_rot,
+        kv,
+        segs,
+        m_s,
+        l_s,
+        acc,
+        send_sems,
+        recv_sems,
+        local_sems,
+    ):
+        at = here()
+        h = at["h"]
+        c = lax.axis_index("ctx")
+        loads = []
+
+        def load(src, dst):
+            copy = pltpu.make_async_copy(src, dst, local_sems.at[len(loads)])
+            copy.start()
+            loads.append(copy)
+
+        load(slots_h, slots_v)
+        for b in range(blocks):
+            load(txt_h.at[b], hid.at[b])
+        for b in range(blocks):
+            load(w_h.at[b], w_v.at[b])
+        load(segr_ref, segs.at[0])
+        greet([ahead(at, s) for s in (1, 2, 3, 4, -1, -2, -3, -4)] + [moved(at, h=1)])
+        net = Net(send_sems, recv_sems, local_sems)
+        partner = moved(at, h=1)
+        sibling = moved(at, k=1)
+        seg_sent = [net.send(segr_ref, segs.at[s], ahead(at, s)) for s in range(1, REACH + 1)]
+        sq[...] = jnp.zeros_like(sq)
+        loads[0].wait()
+        step = 256
+        for b in range(blocks):
+            loads[1 + b].wait()
+
+            @pl.loop(0, tokens // step)
+            def _(r, b=b):
+                rows = pl.ds(pl.multiple_of(r * step, step), step)
+                chosen = table_ref[rows, :]
+                inside = cov_ref[rows, :] > 0.5
+                total = jnp.zeros((step, 1), F32)
+                for n in range(0, width, 512):
+                    filled = jnp.dot(
+                        chosen, slots_v[b, :, n : n + 512], preferred_element_type=F32
+                    )
+                    text = hid[b, rows, n : n + 512].astype(F32)
+                    both = jnp.where(inside, filled, text)
+                    hid[b, rows, n : n + 512] = both.astype(BF)
+                    total = total + jnp.sum(both * both, axis=1, keepdims=True)
+                sq[rows, :] = sq[rows, :] + total
+
+        for b in range(blocks):
+            loads[1 + blocks + b].wait()
+        loads[1 + 2 * blocks].wait()
+        sq_send[...] = jnp.broadcast_to(sq[...], (tokens, 128)).T[:8]
+
+        def project(half, first_col, cols, store):
+            per_row = cols // 256
+
+            @pl.loop(0, (tokens // step) * per_row)
+            def _(i):
+                rows = pl.ds(pl.multiple_of((i // per_row) * step, step), step)
+                inner = pl.multiple_of((i % per_row) * 256, 256)
+                total = None
+                for b in range(blocks):
+                    part = lax.dot_general(
+                        hid[b, rows, :],
+                        w_v[b, half, pl.ds(first_col + inner, 256), :],
+                        (((1,), (1,)), ((), ())),
+                        preferred_element_type=F32,
+                    )
+                    total = part if total is None else total + part
+                store[rows, pl.ds(inner, 256)] = total.astype(store.dtype)
+
+        project(1 - h, qcols, kvcols, kv_send)
+        kv_n = net.send(kv_send, kv_got, partner)
+        sq_n = net.send(sq_send, sq_got, partner)
+        project(1 - h, 0, qcols, q_send)
+        q_n = net.send(q_send, q_got, partner)
+        project(h, qcols, kvcols, kv_keep)
+
+        net.arrived(sq_n)
+        net.arrived(kv_n)
+        other = jnp.broadcast_to(sq_got[:1, :], (128, tokens)).T[:, :1]
+        sq[...] = lax.rsqrt((sq[...] + other) * (1.0 / D) + RMS_EPS)
+
+        def turned(u, rows):
+            return u * cos_ref[rows, :] + pltpu.roll(u, HD // 2, 1) * sin_ref[rows, :]
+
+        @pl.loop(0, tokens // QT)
+        def _(r):
+            rows = pl.ds(pl.multiple_of(r * QT, QT), QT)
+            both = (kv_keep[rows, :] + kv_got[rows, :].astype(F32)) * sq[rows, :]
+            both = both + bias_ref[:, qcols:]
+            kv[0, rows, :HD] = turned(both[:, :HD], rows).astype(BF)
+            kv[0, rows, HD:] = both[:, HD:].astype(BF)
+
+        near = net.send(kv.at[0], kv.at[2], ahead(at, 2))
+        far = net.send(kv.at[0], kv.at[4], ahead(at, 4))
+        project(h, 0, qcols, q_keep)
+        net.arrived(near)
+        one = net.send(kv.at[2 * at["k"]], kv.at[1], sibling)
+        net.arrived(far)
+        three = net.send(kv.at[2 + 2 * at["k"]], kv.at[3], sibling)
+        net.arrived(q_n)
+
+        @pl.loop(0, tokens // QT)
+        def _(r):
+            rows = pl.ds(pl.multiple_of(r * QT, QT), QT)
+            for j in range(GROUP):
+                lanes = slice(j * HD, (j + 1) * HD)
+                u = (q_keep[rows, lanes] + q_got[rows, lanes].astype(F32)) * sq[rows, :]
+                u = u + bias_ref[:, lanes]
+                q_rot[j, rows, :] = turned(u, rows).astype(BF)
+
+        factor = HD ** (-0.5) * 1.4426950408889634
+
+        def attend(d, start):
+            @pl.loop(0, tokens // QT)
+            def _(r):
+                rows = pl.ds(pl.multiple_of(r * QT, QT), QT)
+                key_seg = jnp.where(c >= d, segs[d, :1, :], -1)
+                allowed = segc_ref[rows, :] == key_seg
+                if d == 0:
+                    q_at = lax.broadcasted_iota(jnp.int32, (QT, tokens), 0) + r * QT
+                    k_at = lax.broadcasted_iota(jnp.int32, (QT, tokens), 1)
+                    allowed = allowed & (k_at <= q_at)
+                for j in range(GROUP):
+                    scores = lax.dot_general(
+                        q_rot[j, rows, :],
+                        kv[d, :, :HD],
+                        (((1,), (1,)), ((), ())),
+                        preferred_element_type=F32,
+                    )
+                    scores = jnp.where(allowed, scores * factor, NEG)
+                    top = jnp.max(scores, axis=1, keepdims=True)
+                    if not start:
+                        before = m_s[j, rows, :]
+                        top = jnp.maximum(before, top)
+                    raised = jnp.exp2(scores - top)
+                    total = jnp.sum(raised, axis=1, keepdims=True)
+                    blended = jnp.dot(
+                        raised.astype(BF), kv[d, :, HD:], preferred_element_type=F32
+                    )
+                    if not start:
+                        fade = jnp.exp2(before - top)
+                        total = total + fade * l_s[j, rows, :]
+                        blended = blended + fade * acc[j, rows, :]
+                    m_s[j, rows, :] = top
+                    l_s[j, rows, :] = total
+                    acc[j, rows, :] = blended
+
+        attend(0, True)
+        for n in seg_sent:
+            net.arrived(n)
+        attend(2, False)
+        attend(4, False)
+        net.arrived(one)
+        attend(1, False)
+        net.arrived(three)
+        attend(3, False)
+
+        @pl.loop(0, tokens // QT)
+        def _(r):
+            rows = pl.ds(pl.multiple_of(r * QT, QT), QT)
+            for j in range(GROUP):
+                out_ref[rows, j * HD : (j + 1) * HD] = (
+                    acc[j, rows, :] / l_s[j, rows, :]
+                ).astype(BF)
+
+        net.finish()
+
+    sends = REACH + 3 + 2 + 2
+    vm = pltpu.VMEM
+    spaces = [H, H, H] + [V] * 7
+    return pl.pallas_call(
+        kernel,
+        out_shape=jax.ShapeDtypeStruct((tokens, qcols), BF),
+        in_specs=[pl.BlockSpec(memory_space=s) for s in spaces],
+        out_specs=pl.BlockSpec(memory_space=V),
+        scratch_shapes=[
+            vm(slots.shape, BF),
+            vm(txt_all.shape, BF),
+            vm(weights.shape, BF),
+            vm((tokens, 1), F32),
+            vm((8, tokens), F32),
+            vm((8, tokens), F32),
+            vm((tokens, kvcols), F32),
+            vm((tokens, kvcols), BF),
+            vm((tokens, kvcols), BF),
+            vm((tokens, qcols), F32),
+            vm((tokens, qcols), BF),
+            vm((tokens, qcols), BF),
+            vm((GROUP, tokens, HD), BF),
+            vm((REACH + 1, tokens, kvcols), BF),
+            vm((REACH + 1, 8, tokens), jnp.int32),
+            vm((GROUP, tokens, 1), F32),
+            vm((GROUP, tokens, 1), F32),
+            vm((GROUP, tokens, HD), F32),
+            pltpu.SemaphoreType.DMA((sends,)),
+            pltpu.SemaphoreType.DMA((sends,)),
+            pltpu.SemaphoreType.DMA((2 + 2 * blocks,)),
+        ],
+        compiler_params=pltpu.CompilerParams(
+            collective_id=6, has_side_effects=True, vmem_limit_bytes=60 << 20
+        ),
+        name="finish",
+    )(slots, txt_all, weights, table, covered, bias, cosine, sine, seg_col, seg_row)
 
 
 def softmax_rows(scores, allowed):
@@ -423,12 +620,6 @@
     angles = places[:, None] * frequency[None, :]
     angles = jnp.concatenate([angles, angles], axis=1)
     return (jnp.cos(angles), jnp.sin(angles))
-
-
-def rotary(inputs, cosine, sine):
-    halfway = inputs.shape[-1] // 2
-    turned = jnp.concatenate([-inputs[..., halfway:], inputs[..., :halfway]], axis=-1)
-    return inputs * cosine + turned * sine
 
 
 def pack_tokens(values, positions, span, owners):
@@ -446,19 +637,6 @@
     rows = jnp.concatenate([values, notes.astype(BF)], axis=1)
     packed = jnp.dot(table.astype(BF), rows, preferred_element_type=F32).astype(BF)
     return packed.reshape(owners, CAP, rows.shape[1])
-
-
-def project(hidden, weights):
-    blocks = [
-        lax.dot_general(
-            hidden[b],
-            weights[b],
-            (((1,), (1,)), ((), ())),
-            preferred_element_type=F32,
-        )
-        for b in range(hidden.shape[0])
-    ]
-    return (blocks[0] + blocks[1]) + (blocks[2] + blocks[3])
 
 
 def on_device(
@@ -533,52 +711,22 @@
             for b in range(NY)
         ]
     )
-    covered = jnp.any(table, axis=1)
-    hidden = jnp.where(covered[None, :, None], filled, txt_all)
-    raised = hidden.astype(F32)
-    squares = jnp.sum(raised * raised, axis=(0, 2))
-    weights = llm_all.reshape(NY, -1, width)
-    partial_sum = project(hidden, weights)
-    columns = partial_sum.shape[1] // 2
-    low, high = (partial_sum[:, :columns], partial_sum[:, columns:])
-    keep = jnp.where(is_high, high, low)
-    give = jnp.where(is_high, low, high).astype(BF)
-    square_rows = squares.reshape(-1, 128)
-    got, got_squares = reduce_qkv(give, square_rows)
-    scale = lax.rsqrt((squares + got_squares.reshape(-1)) / D + RMS_EPS)
-    triple = (keep + got.astype(F32)) * scale[:, None] + llm_bias
-
+    covered = jnp.any(table, axis=1, keepdims=True).astype(F32)
     cosine, sine = rope_tables(first, row_count)
-    queries = rotary(
-        triple[:, : GROUP * HD].reshape(row_count, GROUP, HD), cosine[:, None], sine[:, None]
-    ).astype(BF)
-    keys_rot = rotary(triple[:, GROUP * HD : (GROUP + 1) * HD], cosine, sine).astype(BF)
-    values_cut = triple[:, (GROUP + 1) * HD :].astype(BF)
-    kv_all, seg_all = halo(
-        jnp.concatenate([keys_rot, values_cut], axis=1), segments.reshape(-1, 128)
-    )
-    keys_all = kv_all[:, :, :HD].reshape(-1, HD)
-    values_all = kv_all[:, :, HD:].reshape(-1, HD)
-    key_segments = seg_all.reshape(-1)
-    key_places = jnp.concatenate(
-        [
-            first - distance * row_count + jnp.arange(row_count, dtype=jnp.int32)
-            for distance in range(REACH + 1)
-        ],
-        axis=0,
-    )
-    query_places = first + jnp.arange(row_count, dtype=jnp.int32)
-    allowed = (
-        (segments[:, None] == key_segments[None, :])
-        & (key_places[None, :] <= query_places[:, None])
-        & (key_places[None, :] >= 0)
-    )
-    scores = jnp.einsum(
-        "qjd,kd->jqk", queries, keys_all, preferred_element_type=F32
-    ) * HD ** (-0.5)
-    softmaxed = softmax_rows(scores, allowed[None]).astype(BF)
-    blended = jnp.einsum("jqk,kd->qjd", softmaxed, values_all, preferred_element_type=F32)
-    return blended.astype(BF).reshape(row_count, -1)
+    sine = jnp.where(jnp.arange(HD)[None, :] < HD // 2, -sine, sine)
+    seg_row = jnp.broadcast_to(segments[None, :], (8, row_count))
+    return finish(
+        slots,
+        txt_all,
+        llm_all.reshape(NY, 2, -1, width),
+        table.astype(BF),
+        covered,
+        llm_bias,
+        cosine,
+        sine,
+        segments[:, None],
+        seg_row,
+    )
 
 
 def solution(mesh):

time: 329 us -> 291 us (0.88)
  matrix products: 48.1 us -> 11.1 us
  Pallas kernels: 239 us -> 258 us
  other arithmetic: 22.5 us -> 11.9 us
  local copies, waits for them, and re-layouts: 17.1 us -> 8.18 us
    pallas_call x0 -> x1, Pallas kernels: none -> 97.3 us  [finish(): pl.pallas_call(kernel, out_shape=jax.ShapeDtypeStruct((tokens, qcols), BF...]
    pallas_call x7 -> x5, Pallas kernels: 239 us -> 161 us  [exchange(): pl.pallas_call(kernel, out_shape=outs, in_specs=[pl.BlockSpec(memory_spac...]
    dot_general x9 -> x0, matrix products: 24.2 us -> none  [the longest x4 9.34 us: project(): lax.dot_general(hidden[b], weights[b], (((1,), (1,)), ((), ())), preferre...]
    sub x2 -> x1, matrix products: 13.8 us -> 0.99 us  [softmax_rows(): raised = jnp.exp(masked - highest)]
    slice x5 -> x0, local copies, waits for them, and re-layouts: 7.01 us -> none  [the longest x1 3.54 us: project(): weights[b]]
where the time goes in v2:
time: 291 us; the launch traced here: 290 us
  Pallas kernels  258 us (89%)
  other arithmetic  11.9 us (4%)
  matrix products  11.1 us (4%)
  local copies, waits for them, and re-layouts  8.18 us (3%)
    pallas_call x5, Pallas kernels, exchange(): pl.pallas_call(kernel, out_shape=outs, in_specs=[pl.BlockSpec(memory_spac...  161 us
    pallas_call x1, Pallas kernels, finish(): pl.pallas_call(kernel, out_shape=jax.ShapeDtypeStruct((tokens, qcols), BF...  97.3 us

profile of v2, /device:TPU:3, one launch (start us, length us, event | category | flops | bytes accessed | tf_op | source)
XLA Modules:
  0.0 289.9 jit_solution(9650348530455859090)
XLA Ops:
  0.0 1.6 fusion.1
  2.3 0.0 copy-start.2
  2.3 2.6 fusion.10
  5.0 0.0 copy-done.2
  5.0 0.2 broadcast_compare_fusion
  5.2 1.0 fusion.43
  6.2 0.0 copy-start.1
  6.3 1.2 fusion.16
  7.5 0.0 copy-start.5
  7.5 0.0 copy-start
  7.5 0.0 copy-start.4
  7.5 0.0 copy-start.7
  7.6 0.2 copy.32
  7.7 0.9 reshape_reshape.3.refs_0_
  8.6 0.0 copy-done.6
  8.6 0.0 copy-done.1
  8.6 0.1 multiply_convert_fusion.3
  8.7 0.9 copy.33
  9.6 0.0 copy-done.5
  9.6 0.0 copy-done
  9.6 0.0 copy-done.4
  9.6 0.9 multiply_convert_fusion.1
  10.5 0.6 broadcast_in_dim.65.refs_1_
  11.1 36.4 %spread.1 = (bf16[4,128,640]{2,1,0:T(8,128)(2,1)}, s32[4,8,128]{2,1,0:T(8,128)}, bf16[8,256,640]{2,1,0:T(8,128)(2,1)}, f32[4,8,128]{2,1,0:T(8,128)}, bf16[4,2,4,...) custom-call(bf16[128,640]{1,0:T(8,128)(2,1)} %reshape_reshape.3.refs_0_, ...), custom_call_target="tpu_custom_call" | custom-call | tf_op jit(solution)/shard_map/spread/pallas_call | solution.py:109
  47.5 5.1 %convolution_convert_fusion = bf16[512,2048]{1,0:T(8,128)(2,1)} fusion(bf16[512,640]{1,0:T(8,128)(2,1)} %bitcast.91, bf16[2048,640]{1,0:T(8,128)(2,1)} %bitcast.90), kind=kOutput, calls=%fused_computation.4 | convolution fusion | flops 1343225856 | bytes 5373952 | tf_op jit(solution)/shard_map/dot_general | solution.py:681
  52.6 29.7 %reduce_y.1 = (bf16[3,128,2048]{2,1,0:T(8,128)(2,1)}, bf16[4,2,4,4,2,24,1024]{6,5,4,3,2,1,0:T(8,128)(2,1)}) custom-call(bf16[4,128,2048]{2,1,0:T(8,128)(2,1)} %bitcast.73, bf16[4,2,4,4,2,24,1024]{6,5,4,3,2,1,0:T(8,128)(2,1)} %get-tuple-element.24.refs_1_), custom_call_target="tpu_custom_call", output_to_operand_aliasing={{1}: (1, {})} | custom-call | tf_op jit(solution)/shard_map/reduce_y/pallas_call | solution.py:109
  82.3 1.8 convert_reduce_fusion
  84.1 1.2 convert_add_fusion
  85.3 0.8 select_convert_fusion.refs_0_
  86.1 24.9 %reduce_h.1 = (bf16[128,1024]{1,0:T(8,128)(2,1)}, bf16[4,2,4,4,2,24,1024]{6,5,4,3,2,1,0:T(8,128)(2,1)}, bf16[4,512,1024]{2,1,0:T(8,128)(2,1)}) custom-call(bf16[128,1024]{1,0:T(8,128)(2,1)} %select_convert_fusion.refs_0_, bf16[4,2,4,4,2,24,1024]{6,5,4,3,2,1,0:T(8,128)(2,1)} %get-tuple-element.26.refs_1_, ...), custom_call_target="tpu_custom_call", output_to_operand_aliasing={{1}: (1, {}), {2}: (3, {})} | custom-call | tf_op jit(solution)/shard_map/reduce_h/pallas_call | solution.py:109
  111.1 0.7 dynamic-slice_bitcast_fusion
  111.7 1.0 add_convert_fusion
  112.8 0.7 constant_dynamic-slice_fusion
  113.5 0.2 select_convert_fusion.1
  113.7 1.1 fusion.4.refs_0_
  114.9 39.8 %route.1 = (bf16[4,8,8,1152]{3,2,1,0:T(8,128)(2,1)}, bf16[4,2,4,4,2,24,1024]{6,5,4,3,2,1,0:T(8,128)(2,1)}, bf16[4,512,1024]{2,1,0:T(8,128)(2,1)}) custom-call(bf16[32,8,1152]{2,1,0:T(8,128)(2,1)} %fusion.4.refs_0_, bf16[4,2,4,4,2,24,1024]{6,5,4,3,2,1,0:T(8,128)(2,1)} %get-tuple-element.30.refs_1_, ...), custom_call_target="tpu_custom_call", output_to_operand_aliasing={{1}: (1, {}), {2}: (3, {})} | custom-call | tf_op jit(solution)/shard_map/route/pallas_call | solution.py:109
  154.7 29.6 %collect.1 = (bf16[4,4,64,1152]{3,2,1,0:T(8,128)(2,1)}, bf16[4,2,4,4,2,24,1024]{6,5,4,3,2,1,0:T(8,128)(2,1)}) custom-call(bf16[4,64,1152]{2,1,0:T(8,128)(2,1)} %bitcast.80, bf16[4,2,4,4,2,24,1024]{6,5,4,3,2,1,0:T(8,128)(2,1)} %get-tuple-element.33.refs_1_), custom_call_target="tpu_custom_call", output_to_operand_aliasing={{1}: (1, {})} | custom-call | tf_op jit(solution)/shard_map/collect/pallas_call | solution.py:109
  184.3 0.0 copy-start.3
  184.3 0.9 fusion.31
  185.2 0.2 fusion.30
  185.4 0.8 fusion.20
  186.2 0.9 copy.34.cov_ref
  187.1 0.1 broadcast_multiply_fusion
  187.3 2.0 negate_select_fusion
  189.3 0.9 copy.35.segc_ref
  190.1 0.6 broadcast_in_dim.110.segr_ref
  190.7 97.3 %finish.1 = bf16[512,512]{1,0:T(8,128)(2,1)} custom-call(bf16[4,256,1152]{2,1,0:T(8,128)(2,1)} %bitcast.76, bf16[4,512,1024]{2,1,0:T(8,128)(2,1)} %get-tuple-element.35.txt_h, bf16[4,2,768,1024]{3,2,1,0:T(8,128)(2,1)} %bitcast.72, bf16[512,256]{1,0:T(8,128)(2,1)} %get-tuple-element.46.table_ref, f32[512,1]{1,0:T(8,128)} %copy.34.cov_ref, f32[1,768]{1,0:T(1,128)} %bias_ref.1, ...), custom_call_target="tpu_custom_call" | custom-call | tf_op jit(solution)/shard_map/finish/pallas_call | solution.py:550
  288.1 1.9 copy.45
  (16 shorter events, 0.1 us)
Async XLA Ops:
  2.3 2.7 copy-start.2
  6.2 2.4 copy-start.6
  6.2 2.4 copy-start.1
  7.5 2.1 copy-start.5
  7.5 2.1 copy-start
  7.5 2.1 copy-start.4
  7.5 3.0 %copy-start.7 = (s32[128]{0:T(128)S(1)}, s32[128]{0:T(128)}, u32[]{:S(2)}) copy-start(s32[128]{0:T(128)} %param.25) | copy-start | bytes 1540
  184.3 4.9 %copy-start.3 = (s32[512]{0:T(512)S(1)}, s32[512]{0:T(512)}, u32[]{:S(2)}) copy-start(s32[512]{0:T(512)} %param.31) | copy-start | bytes 6148
